TPU v7x, 32 devices: a whole 2x2x4 slice. The times are simulated.
32 devices in a mesh: groups: 2 (over y), ctx: 16 (over z, x, core).
Axes of the slice: x: 2, y: 2, z: 4, core: 2. Of those that a mesh axis runs over, the one named last changes fastest.
Arguments:
- queries: bfloat16 [512, 6144], P(('groups', 'ctx')), parts along dimension 0, may hold values from -8 to 8
- latents: bfloat16 [4096, 576], P(('groups', 'ctx')), parts along dimension 0, may hold values from -8 to 8
- w_uk: bfloat16 [32, 128, 512], replicated, may hold values from -0.5 to 0.5
- w_uv: bfloat16 [32, 512, 128], replicated, may hold values from -1.5 to 1.5
Outputs:
- attended: bfloat16 [512, 4096], P(('groups', 'ctx')), parts along dimension 0
There are 2 independent parts, one for each index of `groups`. A program takes and returns all parts, laid end to end along the dimension named above; an argument that names none is the same for every part. Nothing has to cross between parts.
All inputs are finite; a program needn't handle non-finite values.
Results may differ from a plain program's by a relative error of at most 0.008.
Values may be sent and summed in bfloat16 or wider, within the bound.
No kernel may reach another device: no remote copies, remote signals or barrier semaphores. Data moves between devices by JAX's collectives and lax.ppermute only.
A program may use at most 128 MiB of HBM per device.

v0:
```python
import math
import jax
import jax.numpy as jnp
from jax import lax
from jax.sharding import PartitionSpec as P

NOPE = 128
ROPE = 64
RANK = 512
VDIM = 128


def body(queries, latents, w_uk, w_uv):
    index = lax.axis_index("ctx")
    qrows = queries.shape[0]
    krows = latents.shape[0]
    offset = krows - qrows
    heads = w_uk.shape[0]
    query_pos = index * krows + offset + jnp.arange(qrows, dtype=jnp.int32)
    shaped = queries.reshape(qrows, heads, NOPE + ROPE)
    q_lat = jnp.einsum(
        "thi,hil->thl", shaped[:, :, :NOPE], w_uk, preferred_element_type=jnp.float32
    ).astype(jnp.bfloat16)
    q_rope = shaped[:, :, NOPE:]
    scale = 1.0 / jnp.sqrt(jnp.float32(NOPE + ROPE))
    last_query = jnp.max(query_pos)

    def inner(state, block, kstart):
        sub = block.shape[0]
        kpos = kstart + jnp.arange(sub, dtype=jnp.int32)

        def work(carried):
            running, total, acc = carried
            score = jnp.einsum(
                "thl,jl->thj", q_lat, block[:, :RANK], preferred_element_type=jnp.float32
            )
            score = score + jnp.einsum(
                "thr,jr->thj", q_rope, block[:, RANK:], preferred_element_type=jnp.float32
            )
            score = score * scale
            allowed = kpos[None, None, :] <= query_pos[:, None, None]
            score = jnp.where(allowed, score, -jnp.inf)
            fresh = jnp.maximum(running, jnp.max(score, axis=-1))
            expo = jnp.exp(score - fresh[:, :, None])
            factor = jnp.exp(running - fresh)
            total = total * factor + jnp.sum(expo, axis=-1)
            acc = acc * factor[:, :, None] + jnp.einsum(
                "thj,jl->thl",
                expo.astype(jnp.bfloat16),
                block[:, :RANK],
                preferred_element_type=jnp.float32,
            )
            return (fresh, total, acc)

        return lax.cond(kstart > last_query, lambda carried: carried, work, state)

    def accumulate(carry, piece, start):
        count = piece.shape[0]
        sub = math.gcd(count, 2048)
        if sub == count:
            return inner(carry, piece, start)
        blocks = piece.reshape(count // sub, sub, piece.shape[1])
        starts = start + jnp.arange(count // sub, dtype=jnp.int32) * sub

        def step(state, items):
            return (inner(state, items[0], items[1]), None)

        result, unused = lax.scan(step, carry, (blocks, starts))
        return result

    init = (
        jnp.full((qrows, heads), -1e30, jnp.float32),
        jnp.zeros((qrows, heads), jnp.float32),
        jnp.zeros((qrows, heads, RANK), jnp.float32),
    )
    running, total, acc = accumulate(
        init, lax.all_gather(latents, "ctx", axis=0, tiled=True), jnp.int32(0)
    )
    o_lat = (acc / total[:, :, None]).astype(jnp.bfloat16)
    result = jnp.einsum("thl,hlc->thc", o_lat, w_uv, preferred_element_type=jnp.float32).astype(
        jnp.bfloat16
    )
    result = result.reshape(qrows, heads * VDIM)
    return result


def solution(mesh):
    placed = (P(("groups", "ctx"), None), P(("groups", "ctx"), None), P(), P())
    return jax.shard_map(
        body, mesh=mesh, in_specs=placed, out_specs=P(("groups", "ctx"), None), check_vma=False
    )
```

profile of v0, /device:TPU:0, one launch (start us, length us, event | category | flops | bytes accessed | tf_op | source)
XLA Modules:
  0.0 76.3 jit_solution(9675604063775418156)
XLA Ops:
  6.5 0.0 all-gather.2.cloned.1.call-start
  6.5 1.7 %copy.11 = bf16[128,576]{1,0:T(8,128)(2,1)} copy(bf16[128,576]{0,1:T(8,128)(2,1)} %param.7) | data formatting | bytes 294912 | tf_op args[1]
  8.2 0.0 all-gather.2.cloned.1.call-update
  8.3 0.6 fusion.22
  9.6 1.3 %reshape.42 = bf16[16,32,192]{2,1,0:T(8,128)(2,1)S(1)} reshape(bf16[16,6144]{1,0:T(8,128)(2,1)} %param.6) | data formatting | bytes 393216 | tf_op jit(solution)/shard_map/reshape | solution.py:20
  10.9 2.9 %fusion.18 = bf16[16,32,512]{2,0,1:T(8,128)(2,1)S(1)} fusion(bf16[32,128,512]{2,1,0:T(8,128)(2,1)} %param.8, bf16[16,32,128]{2,1,0:T(8,128)(2,1)S(1)} %slice.16), kind=kOutput, calls=%fused_computation.20 | convolution fusion | flops 67371008 | bytes 4849664 | tf_op jit(solution)/shard_map/thi,hil->thl/dot_general | solution.py:21
  13.7 41.7 %all-gather.2.cloned.1.call-done = bf16[2048,576]{1,0:T(8,128)(2,1)} async-done(((bf16[128,576]{1,0:T(8,128)(2,1)}), bf16[2048,576]{1,0:T(8,128)(2,1)}) %all-gather.2.cloned.1.call-update) | async-done | bytes 2359312 | tf_op jit(solution)/shard_map/all_gather | solution.py:77
  55.4 10.1 %conditional.1 = (f32[16,32]{1,0:T(8,128)S(1)}, f32[16,32,512]{2,1,0:T(8,128)S(1)}) conditional(s32[]{:T(128)} %convert_element_type.21, (s32[2048]{0:T(1024)S(1)}, s32[16]{0:T(128)S(1)}, bf16[2048,576]{1,0:T(8,128)(2,1)}, bf16[16,32,512]{2,0,1:T(8,128)(2,1)S(1)}, bf16[16,32,192]{2,1,0:T(8,128)(2,1)S(1)}) %tuple.13, () %tuple.14), branch_computations={%region_1.4_spmd, %region_4.5_spmd} | conditional | flops 2290386432 | bytes 41396332 | solution.py:55
  55.4 0.0 copy-start
  55.4 0.1 broadcast_compare_fusion
  55.5 4.6 %copy.10 = bf16[2048,576]{0,1:T(8,128)(2,1)} copy(bf16[2048,576]{1,0:T(8,128)(2,1)} %get-tuple-element.19) | data formatting | bytes 4718592 | tf_op jit(solution)/shard_map
  60.1 0.0 copy-done
  60.1 1.4 %fusion.5 = f32[16,32,2048]{2,1,0:T(8,128)S(1)} fusion(bf16[2048,576]{1,0:T(8,128)(2,1)S(1)} %copy-done, bf16[16,32,512]{2,0,1:T(8,128)(2,1)S(1)} %get-tuple-element.33), kind=kOutput, calls=%fused_computation.6 | convolution fusion | flops 1073741824 | bytes 6815744 | tf_op jit(solution)/shard_map/cond/branch_0_fun/thl,jl->thj/dot_general | solution.py:34
  61.5 2.0 %fusion.23 = (f32[16,32]{1,0:T(8,128)S(1)}, f32[16,32,2048]{2,1,0:T(8,128)S(1)}) fusion(f32[16,32,2048]{2,1,0:T(8,128)S(1)} %fusion.5, bf16[2048,576]{0,1:T(8,128)(2,1)} %copy.10, bf16[16,32,192]{2,1,0:T(8,128)(2,1)S(1)} %get-tuple-element.20, pred[16,2048]{1,0:T(8,128)(4,1)S(1)} %broadcast_compare_fusion), kind=kOutput, calls=%fused_computation.29 | convolution fusion | flops 138411520 | bytes 8816640 | tf_op jit(solution)/shard_map/cond/branch_0_fun/thr,jr->thj/dot_general | solution.py:37
  63.4 0.7 fusion.1
  64.2 1.3 %fusion.10 = f32[16,32,512]{2,1,0:T(8,128)S(1)} fusion(bf16[2048,576]{1,0:T(8,128)(2,1)S(1)} %copy-done, f32[16,32,2048]{2,1,0:T(8,128)S(1)} %get-tuple-element.38, f32[16,32]{1,0:T(8,128)S(1)} %broadcast_maximum_fusion, f32[16,32]{1,0:T(8,128)S(1)} %get-tuple-element.35), kind=kOutput, calls=%fused_computation.11 | convolution fusion | flops 1076101120 | bytes 7356416 | tf_op jit(solution)/shard_map/cond/branch_0_fun/thj,jl->thl/dot_general | solution.py:47
  65.5 0.1 divide_convert_fusion
  65.7 3.1 %fusion.19 = bf16[32,2,8,128]{3,2,1,0:T(8,128)(2,1)S(1)} fusion(bf16[32,512,128]{2,1,0:T(8,128)(2,1)} %param.9, bf16[16,32,512]{2,1,0:T(8,128)(2,1)S(1)} %divide_convert_fusion), kind=kOutput, calls=%fused_computation.22 | convolution fusion | flops 67174400 | bytes 4849664 | tf_op jit(solution)/shard_map/thl,hlc->thc/dot_general | solution.py:80
  68.7 0.7 copy.25
  (5 shorter events, 0.1 us)
Async XLA Ops:
  6.5 48.9 %all-gather.2.cloned.1.call-start = ((), (), s32[]{:S(2)}) async-start(), calls=%async_computation | async-start | bytes 2785280 | tf_op jit(solution)/shard_map/all_gather | solution.py:77
  55.4 4.6 %copy-start = (bf16[2048,576]{1,0:T(8,128)(2,1)S(1)}, bf16[2048,576]{1,0:T(8,128)(2,1)}, u32[]{:S(2)}) copy-start(bf16[2048,576]{1,0:T(8,128)(2,1)} %get-tuple-element.19) | copy-start | bytes 7077892 | tf_op jit(solution)/shard_map/cond
Sparse Core Ops, SparseCore 0:
  9.6 45.7 all-gather.1
where the time goes:
time: 76.6 us; the launch traced here: 76.3 us
  waiting for transfers between devices  41.7 us (54%)
  between operations  14.1 us (18%)
  matrix products  10.6 us (14%)
  local copies, waits for them, and re-layouts  8.22 us (11%)
  other arithmetic  1.61 us (2%)
    all_gather x1, waiting for transfers between devices, body(): lax.all_gather(latents, 'ctx', axis=0, tiled=True)  41.7 us
    another operation x1, local copies, waits for them, and re-layouts  4.55 us
    dot_general x1, matrix products, body(): jnp.einsum('thl,hlc->thc', o_lat, w_uv, preferred_element_type=jnp.float32)  3.07 us
    dot_general x1, matrix products, body(): jnp.einsum('thi,hil->thl', shaped[:, :, :NOPE], w_uk, preferred_element_t...  2.86 us
    dot_general x1, matrix products, work(): jnp.einsum('thr,jr->thj', q_rope, block[:, RANK:], preferred_element_type...  1.96 us
    unnamed x1, local copies, waits for them, and re-layouts  1.7 us
  transfers between devices with their start and end apart: 1, of which 1 were waited for; matrix products, arithmetic and copies ran while one was open for 6% of the time, Pallas kernels for 0%

commit v1 on v0

--- a/solution.py
+++ b/solution.py
@@ -8,6 +8,14 @@
 ROPE = 64
 RANK = 512
 VDIM = 128
+
+
+def gather_by_exchange(shard, axis, dim):
+    size = lax.axis_size(axis)
+    repeats = [size if d == dim else 1 for d in range(shard.ndim)]
+    return lax.all_to_all(
+        jnp.tile(shard, repeats), axis, split_axis=dim, concat_axis=dim, tiled=True
+    )
 
 
 def body(queries, latents, w_uk, w_uv):
@@ -73,9 +81,7 @@
         jnp.zeros((qrows, heads), jnp.float32),
         jnp.zeros((qrows, heads, RANK), jnp.float32),
     )
-    running, total, acc = accumulate(
-        init, lax.all_gather(latents, "ctx", axis=0, tiled=True), jnp.int32(0)
-    )
+    running, total, acc = accumulate(init, gather_by_exchange(latents, "ctx", 0), jnp.int32(0))
     o_lat = (acc / total[:, :, None]).astype(jnp.bfloat16)
     result = jnp.einsum("thl,hlc->thc", o_lat, w_uv, preferred_element_type=jnp.float32).astype(
         jnp.bfloat16

time: 76.6 us -> 75.7 us (0.988)
  the two profiles are of different devices: /device:TPU:0 before, /device:TPU:11 now
where the time goes in v1:
time: 75.7 us; the launch traced here: 75.4 us
  waiting for transfers between devices  48.5 us (64%)
  matrix products  9.64 us (13%)
  local copies, waits for them, and re-layouts  8.33 us (11%)
  starting transfers between devices  6.52 us (9%)
  other arithmetic  1.61 us (2%)
    all_to_all x1, waiting for transfers between devices, gather_by_exchange(): lax.all_to_all(jnp.tile(shard, repeats), axis, split_axis=dim, concat_axi...  48.5 us
    all_to_all x1, starting transfers between devices, gather_by_exchange(): lax.all_to_all(jnp.tile(shard, repeats), axis, split_axis=dim, concat_axi...  6.52 us
    another operation x1, local copies, waits for them, and re-layouts  3.09 us
    dot_general x1, matrix products, body(): jnp.einsum('thl,hlc->thc', o_lat, w_uv, preferred_element_type=jnp.float32)  3.07 us
    dot_general x1, matrix products, body(): jnp.einsum('thi,hil->thl', shaped[:, :, :NOPE], w_uk, preferred_element_t...  2.83 us
    another operation x1, local copies, waits for them, and re-layouts, gather_by_exchange(): jnp.tile(shard, repeats)  2.82 us
  transfers between devices with their start and end apart: 1, of which 1 were waited for; matrix products, arithmetic and copies ran while one was open for 5% of the time, Pallas kernels for 0%

profile of v1, /device:TPU:11, one launch (start us, length us, event | category | flops | bytes accessed | tf_op | source)
XLA Modules:
  0.0 75.4 jit_solution(53422086097092464)
XLA Ops:
  0.0 0.0 copy-start.1
  0.0 2.8 %tile.2 = bf16[16,128,576]{1,2,0:T(8,128)(2,1)} broadcast(bf16[128,576]{0,1:T(8,128)(2,1)} %param.7), dimensions={1,2} | broadcast | bytes 2506752 | tf_op jit(solution)/shard_map/tile | solution.py:17
  2.8 6.5 %all-to-all-start = ((bf16[16,128,576]{1,2,0:T(8,128)(2,1)}), bf16[16,128,576]{1,2,0:T(8,128)(2,1)S(1)}, u32[]{:S(2)}, u32[]{:S(2)}) async-start(bf16[16,128,576]{1,2,0:T(8,128)(2,1)} %tile.2), calls=%async_computation | async-start | bytes 4718592 | tf_op jit(solution)/shard_map/all_to_all | solution.py:16
  9.3 0.6 fusion.16
  10.6 0.0 copy-done.1
  10.6 0.3 reshape.50
  11.0 2.8 %fusion.12 = bf16[16,32,512]{2,0,1:T(8,128)(2,1)S(1)} fusion(bf16[32,128,512]{2,1,0:T(8,128)(2,1)} %param.8, bf16[16,32,128]{2,1,0:T(8,128)(2,1)S(1)} %slice.17), kind=kOutput, calls=%fused_computation.17 | convolution fusion | flops 67371008 | bytes 4849664 | tf_op jit(solution)/shard_map/thi,hil->thl/dot_general | solution.py:29
  13.8 48.5 %all-to-all-done = bf16[16,128,576]{1,2,0:T(8,128)(2,1)S(1)} async-done(((bf16[16,128,576]{1,2,0:T(8,128)(2,1)}), bf16[16,128,576]{1,2,0:T(8,128)(2,1)S(1)}, u32[]{:S(2)}, u32[]{:S(2)}) %all-to-all-start) | async-done | bytes 2359328 | tf_op jit(solution)/shard_map/all_to_all | solution.py:16
  62.4 9.1 %conditional.1 = (f32[16,32]{1,0:T(8,128)S(1)}, f32[16,32,512]{2,1,0:T(8,128)S(1)}) conditional(s32[]{:T(128)} %convert_element_type.21, (s32[2048]{0:T(1024)S(1)}, s32[16]{0:T(128)S(1)}, bf16[16,128,576]{1,2,0:T(8,128)(2,1)S(1)}, bf16[16,32,512]{2,0,1:T(8,128)(2,1)S(1)}, bf16[16,32,192]{2,1,0:T(8,128)(2,1)S(1)}) %tuple.13, () %tuple.14), branch_computations={%region_1.4_spmd, %region_4.5_spmd} | conditional | flops 2290386432 | bytes 41658476 | solution.py:63
  62.4 0.0 copy-start
  62.4 1.4 %copy-done = bf16[16,128,576]{1,2,0:T(8,128)(2,1)} copy-done((bf16[16,128,576]{1,2,0:T(8,128)(2,1)}, bf16[16,128,576]{1,2,0:T(8,128)(2,1)S(1)}, u32[]{:S(2)}) %copy-start) | copy-done | bytes 2359320 | tf_op jit(solution)/shard_map/cond
  63.8 0.1 broadcast_compare_fusion
  63.9 3.1 %copy.18 = bf16[16,128,576]{2,1,0:T(8,128)(2,1)S(1)} copy(bf16[16,128,576]{1,2,0:T(8,128)(2,1)} %copy-done) | data formatting | bytes 4718592 | tf_op jit(solution)/shard_map
  67.0 1.4 %fusion.5 = f32[16,32,2048]{2,1,0:T(8,128)S(1)} fusion(bf16[2048,576]{1,0:T(8,128)(2,1)S(1)} %bitcast.22, bf16[16,32,512]{2,0,1:T(8,128)(2,1)S(1)} %get-tuple-element.39), kind=kOutput, calls=%fused_computation.7 | convolution fusion | flops 1073741824 | bytes 6815744 | tf_op jit(solution)/shard_map/cond/branch_0_fun/thl,jl->thj/dot_general | solution.py:42
  68.3 1.0 %fusion.17 = (f32[16,32]{1,0:T(8,128)S(1)}, f32[16,32,2048]{2,1,0:T(8,128)S(1)}) fusion(f32[16,32,2048]{2,1,0:T(8,128)S(1)} %fusion.5, bf16[2048,576]{1,0:T(8,128)(2,1)S(1)} %bitcast.23, bf16[16,32,192]{2,1,0:T(8,128)(2,1)S(1)} %get-tuple-element.21, pred[16,2048]{1,0:T(8,128)(4,1)S(1)} %broadcast_compare_fusion), kind=kOutput, calls=%fused_computation.26 | convolution fusion | flops 138411520 | bytes 9078784 | tf_op jit(solution)/shard_map/cond/branch_0_fun/thr,jr->thj/dot_general | solution.py:45
  69.4 0.7 fusion.1
  70.1 1.3 %fusion.6 = f32[16,32,512]{2,1,0:T(8,128)S(1)} fusion(bf16[2048,576]{1,0:T(8,128)(2,1)S(1)} %bitcast.24, f32[16,32,2048]{2,1,0:T(8,128)S(1)} %get-tuple-element.44, f32[16,32]{1,0:T(8,128)S(1)} %broadcast_maximum_fusion, f32[16,32]{1,0:T(8,128)S(1)} %get-tuple-element.41), kind=kOutput, calls=%fused_computation.8 | convolution fusion | flops 1076101120 | bytes 7356416 | tf_op jit(solution)/shard_map/cond/branch_0_fun/thj,jl->thl/dot_general | solution.py:55
  71.5 0.1 divide_convert_fusion
  71.6 3.1 %fusion.13 = bf16[32,2,8,128]{3,2,1,0:T(8,128)(2,1)S(1)} fusion(bf16[32,512,128]{2,1,0:T(8,128)(2,1)} %param.9, bf16[16,32,512]{2,1,0:T(8,128)(2,1)S(1)} %divide_convert_fusion), kind=kOutput, calls=%fused_computation.19 | convolution fusion | flops 67174400 | bytes 4849664 | tf_op jit(solution)/shard_map/thl,hlc->thc/dot_general | solution.py:86
  74.7 0.7 copy.33
  (5 shorter events, 0.0 us)
Async XLA Ops:
  0.0 10.6 %copy-start.1 = (bf16[16,6144]{1,0:T(8,128)(2,1)S(1)}, bf16[16,6144]{1,0:T(8,128)(2,1)}, u32[]{:S(2)}) copy-start(bf16[16,6144]{1,0:T(8,128)(2,1)} %param.6) | copy-start | bytes 589828
  2.8 59.6 %all-to-all-start = ((bf16[16,128,576]{1,2,0:T(8,128)(2,1)}), bf16[16,128,576]{1,2,0:T(8,128)(2,1)S(1)}, u32[]{:S(2)}, u32[]{:S(2)}) async-start(bf16[16,128,576]{1,2,0:T(8,128)(2,1)} %tile.2), calls=%async_computation | async-start | bytes 4718592 | tf_op jit(solution)/shard_map/all_to_all | solution.py:16
  62.4 1.4 %copy-start = (bf16[16,128,576]{1,2,0:T(8,128)(2,1)}, bf16[16,128,576]{1,2,0:T(8,128)(2,1)S(1)}, u32[]{:S(2)}) copy-start(bf16[16,128,576]{1,2,0:T(8,128)(2,1)S(1)} %get-tuple-element.38) | copy-start | bytes 7077892 | tf_op jit(solution)/shard_map/cond
